TPU v7x, 32 devices: a whole 2x2x4 slice. The times are simulated.
32 devices in a mesh: dp: 8 (over y, x, core), seq: 4 (over z).
Axes of the slice: x: 2, y: 2, z: 4, core: 2. Of those that a mesh axis runs over, the one named last changes fastest.
Arguments:
- layer_input: bfloat16 [8, 1024, 2048], P('dp', 'seq'), may hold values from -6 to 6
- segments: int32 [8, 1024], P('dp'), may hold values from 0 to 3, never falling along the last dimension, each value on 1 to 512 neighbouring positions
- w_query: bfloat16 [2048, 2048], P(('dp', 'seq')), may hold values from -0.125 to 0.125
- w_key: bfloat16 [2048, 2048], P(('dp', 'seq')), may hold values from -0.125 to 0.125
- w_value: bfloat16 [2048, 2048], P(('dp', 'seq')), may hold values from -0.125 to 0.125
- w_output: bfloat16 [2048, 2048], P(('dp', 'seq')), may hold values from -0.125 to 0.125
- w_gate: bfloat16 [2048, 8192], P(('dp', 'seq')), may hold values from -0.125 to 0.125
- w_up: bfloat16 [2048, 8192], P(('dp', 'seq')), may hold values from -0.125 to 0.125
- w_down: bfloat16 [8192, 2048], P(None, ('dp', 'seq')), may hold values from -0.0625 to 0.0625
- query_gain: float32 [2048], replicated, may hold values from 0.1 to 1.9
- key_gain: float32 [2048], replicated, may hold values from 0.1 to 1.9
- attn_gain: float32 [2048], replicated, may hold values from 0.1 to 1.9
- ff_gain: float32 [2048], replicated, may hold values from 0.1 to 1.9
- cotangent: bfloat16 [8, 1024, 2048], P('dp', 'seq'), may hold values from -6 to 6
Outputs:
- activation: bfloat16 [8, 1024, 2048], P('dp', 'seq')
- input_grad: bfloat16 [8, 1024, 2048], P('dp', 'seq')
- grad_query: float32 [2048, 2048], P(('dp', 'seq'))
- grad_key: float32 [2048, 2048], P(('dp', 'seq'))
- grad_value: float32 [2048, 2048], P(('dp', 'seq'))
- grad_output: float32 [2048, 2048], P(('dp', 'seq'))
- grad_gate: float32 [2048, 8192], P(('dp', 'seq'))
- grad_up: float32 [2048, 8192], P(('dp', 'seq'))
- grad_down: float32 [8192, 2048], P(None, ('dp', 'seq'))
- grad_query_gain: float32 [2048], P(('dp', 'seq'))
- grad_key_gain: float32 [2048], P(('dp', 'seq'))
- grad_attn_gain: float32 [2048], P(('dp', 'seq'))
- grad_ff_gain: float32 [2048], P(('dp', 'seq'))
Inputs may be any that keep to these rules, and one draw needn't show every extreme that they name: `segments`: segment numbers never fall along a row, and a document holds at most half of 1024 tokens.
All inputs are finite; a program needn't handle non-finite values.
Results may differ from a plain program's by a relative error of at most 0.017.
Values may be sent and summed in bfloat16 or wider, within the bound.
No kernel may reach another device: no remote copies, remote signals or barrier semaphores. Data moves between devices by JAX's collectives and lax.ppermute only.
A program may use at most 384 MiB of HBM per device.

v0:
```python
import jax
import jax.numpy as jnp
from jax import lax
from jax.sharding import PartitionSpec as P

HD = 128
EPSILON = 1e-06
ROPE_BASE = 500000.0
MASKED = -1e30


def rms_norm(values, gain_vec):
    factor = lax.rsqrt(jnp.mean(values * values, axis=-1, keepdims=True) + EPSILON)
    return values * factor * gain_vec


def rope_tables(positions):
    half_dim = HD // 2
    frequency = jnp.power(
        jnp.float32(ROPE_BASE), -jnp.arange(half_dim, dtype=jnp.float32) * (2.0 / HD)
    )
    angles = positions[:, None] * frequency[None, :]
    angles = jnp.concatenate([angles, angles], axis=-1)
    return (jnp.cos(angles), jnp.sin(angles))


def rotate(values, cosine_table, sine_table):
    shaped = values.reshape(values.shape[:-1] + (values.shape[-1] // HD, HD))
    first_half = shaped[..., : HD // 2]
    second = shaped[..., HD // 2 :]
    turned = jnp.concatenate([-second, first_half], axis=-1)
    rotated = shaped * cosine_table[:, None, :] + turned * sine_table[:, None, :]
    return rotated.reshape(values.shape)


def project(left, weight):
    return jnp.dot(left, weight, preferred_element_type=jnp.float32)


def back_project(grad_in, weight):
    return lax.dot_general(
        grad_in, weight, (((grad_in.ndim - 1,), (1,)), ((), ())), preferred_element_type=jnp.float32
    )


def rows_product(left, right):
    return lax.dot_general(
        left, right, (((0,), (0,)), ((), ())), preferred_element_type=jnp.float32
    )


def block_mask(segments, row_start, block_rows):
    seq_length = segments.shape[1]
    query_pos = row_start + jnp.arange(block_rows, dtype=jnp.int32)
    query_seg = lax.dynamic_slice_in_dim(segments, row_start, block_rows, 1)
    key_pos = jnp.arange(seq_length, dtype=jnp.int32)
    causal = key_pos[None, None, :] <= query_pos[None, :, None]
    return causal & (segments[:, None, :] == query_seg[:, :, None])


def block_scores(query_block, key_heads, segments, row_start, block_rows):
    score_scale = HD ** (-0.5)
    scores = (
        jnp.einsum("rqhd,rkhd->rhqk", query_block, key_heads, preferred_element_type=jnp.float32)
        * score_scale
    )
    allowed = block_mask(segments, row_start, block_rows)
    return jnp.where(allowed[:, None], scores, MASKED)


def attend(query_all, key_all, value_all, segments):
    row_count, seq_length, local_width = query_all.shape
    head_count = local_width // HD
    block_rows = min(512, seq_length)
    block_count = seq_length // block_rows
    query_split = query_all.reshape(row_count, block_count, block_rows, head_count, HD)
    key_heads = key_all.reshape(row_count, seq_length, head_count, HD)
    value_heads = value_all.reshape(row_count, seq_length, head_count, HD)

    def one_block(block_index):
        query_block = lax.dynamic_index_in_dim(query_split, block_index, 1, keepdims=False)
        scores = block_scores(
            query_block, key_heads, segments, block_index * block_rows, block_rows
        )
        top_score = jnp.max(scores, axis=-1, keepdims=True)
        exp_scores = jnp.exp(scores - top_score)
        row_total = jnp.sum(exp_scores, axis=-1, keepdims=True)
        probs_full = exp_scores / row_total
        log_total = top_score + jnp.log(row_total)
        mixed = jnp.einsum(
            "rhqk,rkhd->rqhd",
            probs_full.astype(jnp.bfloat16),
            value_heads,
            preferred_element_type=jnp.float32,
        )
        return (mixed.astype(jnp.bfloat16), log_total[..., 0])

    mixed_blocks, log_totals = lax.map(one_block, jnp.arange(block_count, dtype=jnp.int32))
    mixed_all = jnp.moveaxis(mixed_blocks, 0, 1).reshape(row_count, seq_length, local_width)
    return (mixed_all, log_totals)


def attend_back(query_all, key_all, value_all, grad_mixed, log_totals, segments):
    row_count, seq_length, local_width = query_all.shape
    head_count = local_width // HD
    block_rows = min(512, seq_length)
    block_count = seq_length // block_rows
    score_scale = HD ** (-0.5)
    query_split = query_all.reshape(row_count, block_count, block_rows, head_count, HD)
    grad_split = grad_mixed.reshape(row_count, block_count, block_rows, head_count, HD)
    key_heads = key_all.reshape(row_count, seq_length, head_count, HD)
    value_heads = value_all.reshape(row_count, seq_length, head_count, HD)

    def one_block(totals, step_item):
        block_index, log_total = step_item
        grad_keys, grad_values = totals
        query_block = lax.dynamic_index_in_dim(query_split, block_index, 1, keepdims=False)
        grad_block = lax.dynamic_index_in_dim(grad_split, block_index, 1, keepdims=False)
        scores = block_scores(
            query_block, key_heads, segments, block_index * block_rows, block_rows
        )
        probs_full = jnp.exp(scores - log_total[..., None])
        grad_probs = jnp.einsum(
            "rqhd,rkhd->rhqk", grad_block, value_heads, preferred_element_type=jnp.float32
        )
        grad_values = grad_values + jnp.einsum(
            "rhqk,rqhd->rkhd",
            probs_full.astype(jnp.bfloat16),
            grad_block,
            preferred_element_type=jnp.float32,
        )
        inner = jnp.sum(probs_full * grad_probs, axis=-1, keepdims=True)
        grad_scores = (probs_full * (grad_probs - inner)).astype(jnp.bfloat16)
        grad_query = (
            jnp.einsum(
                "rhqk,rkhd->rqhd", grad_scores, key_heads, preferred_element_type=jnp.float32
            )
            * score_scale
        )
        grad_keys = (
            grad_keys
            + jnp.einsum(
                "rhqk,rqhd->rkhd", grad_scores, query_block, preferred_element_type=jnp.float32
            )
            * score_scale
        )
        return ((grad_keys, grad_values), grad_query.astype(jnp.bfloat16))

    zeros_heads = jnp.zeros((row_count, seq_length, head_count, HD), jnp.float32)
    (grad_keys, grad_values), grad_queries = lax.scan(
        one_block,
        (zeros_heads, zeros_heads),
        (jnp.arange(block_count, dtype=jnp.int32), log_totals),
    )
    grad_queries = jnp.moveaxis(grad_queries, 0, 1).reshape(row_count, seq_length, local_width)
    grad_keys = grad_keys.reshape(row_count, seq_length, local_width).astype(jnp.bfloat16)
    grad_values = grad_values.reshape(row_count, seq_length, local_width).astype(jnp.bfloat16)
    return (grad_queries, grad_keys, grad_values)


def silu_mix(gate_in, up_in):
    return jax.nn.silu(gate_in) * up_in


def shards(
    layer_input,
    segments,
    w_query,
    w_key,
    w_value,
    w_output,
    w_gate,
    w_up,
    w_down,
    query_gain,
    key_gain,
    attn_gain,
    ff_gain,
    cotangent,
):
    row_count, local_len, model_width = layer_input.shape
    offset = lax.axis_index("seq") * local_len
    positions = (offset + jnp.arange(local_len, dtype=jnp.int32)).astype(jnp.float32)
    cosine_table, sine_table = rope_tables(positions)

    def front(values, gain_vec):
        return rotate(rms_norm(values, gain_vec), cosine_table, sine_table)

    wq_all, wk_all, wv_all, wo_all = (
        lax.all_gather(w_query, ("dp", "seq"), axis=0, tiled=True),
        lax.all_gather(w_key, ("dp", "seq"), axis=0, tiled=True),
        lax.all_gather(w_value, ("dp", "seq"), axis=0, tiled=True),
        lax.all_gather(w_output, ("dp", "seq"), axis=0, tiled=True),
    )
    q_proj = project(layer_input, wq_all)
    k_proj = project(layer_input, wk_all)
    v_proj = project(layer_input, wv_all)
    q_rot, query_back = jax.vjp(front, q_proj, query_gain)
    k_rot, key_back = jax.vjp(front, k_proj, key_gain)
    q_low = q_rot.astype(jnp.bfloat16)
    k_low = k_rot.astype(jnp.bfloat16)
    v_low = v_proj.astype(jnp.bfloat16)
    q_heads, k_heads, v_heads = (
        lax.all_to_all(q_low, "seq", split_axis=2, concat_axis=1, tiled=True),
        lax.all_to_all(k_low, "seq", split_axis=2, concat_axis=1, tiled=True),
        lax.all_to_all(v_low, "seq", split_axis=2, concat_axis=1, tiled=True),
    )
    mixed_heads, log_totals = attend(q_heads, k_heads, v_heads, segments)
    mixed_local = lax.all_to_all(mixed_heads, "seq", split_axis=1, concat_axis=2, tiled=True)
    attn_out = project(mixed_local, wo_all)
    attn_normed, attn_back = jax.vjp(rms_norm, attn_out, attn_gain)
    residual = layer_input.astype(jnp.float32) + attn_normed
    residual_low = residual.astype(jnp.bfloat16)
    grad_top = cotangent.astype(jnp.float32)
    gate_part, up_part, down_part = (
        lax.all_to_all(w_gate, "seq", split_axis=1, concat_axis=0, tiled=True),
        lax.all_to_all(w_up, "seq", split_axis=1, concat_axis=0, tiled=True),
        lax.all_to_all(w_down.T, "seq", split_axis=1, concat_axis=0, tiled=True),
    )
    wg_blk, wu_blk, wd_blk = (
        lax.all_gather(gate_part, "dp", axis=0, tiled=True),
        lax.all_gather(up_part, "dp", axis=0, tiled=True),
        lax.all_gather(down_part, "dp", axis=0, tiled=True),
    )
    resid_full, cot_full = (
        lax.all_gather(residual_low, "seq", axis=1, tiled=True),
        lax.all_gather(cotangent, "seq", axis=1, tiled=True),
    )
    gate_act = project(resid_full, wg_blk)
    up_act = project(resid_full, wu_blk)
    hidden_low = silu_mix(gate_act, up_act).astype(jnp.bfloat16)
    ff_full = lax.psum(back_project(hidden_low, wd_blk).astype(jnp.bfloat16), "seq").astype(
        jnp.float32
    )
    ff_own = lax.dynamic_slice_in_dim(ff_full, offset, local_len, 1)
    ff_normed, ff_back = jax.vjp(rms_norm, ff_own, ff_gain)
    activation = (residual + ff_normed).astype(jnp.bfloat16)
    _, grad_ffg = ff_back(grad_top)
    _, full_back = jax.vjp(rms_norm, ff_full, ff_gain)
    grad_ff32, _ = full_back(cot_full.astype(jnp.float32))
    grad_ff = grad_ff32.astype(jnp.bfloat16)
    grad_hidden = project(grad_ff, wd_blk)
    _, mix_back = jax.vjp(silu_mix, gate_act, up_act)
    grad_gate32, grad_up32 = mix_back(grad_hidden)
    grad_gate_low = grad_gate32.astype(jnp.bfloat16)
    grad_up_low = grad_up32.astype(jnp.bfloat16)
    partial_resid = back_project(grad_gate_low, wg_blk) + back_project(grad_up_low, wu_blk)
    grad_resid = grad_top + lax.psum_scatter(partial_resid, "seq", scatter_dimension=1, tiled=True)
    residual_flat = resid_full.reshape(-1, model_width)
    grad_ff_flat = grad_ff.reshape(-1, model_width)
    hidden_flat = hidden_low.reshape(-1, hidden_low.shape[-1])
    grad_gate_flat = grad_gate_low.reshape(-1, hidden_low.shape[-1])
    grad_up_flat = grad_up_low.reshape(-1, hidden_low.shape[-1])
    block_width = hidden_low.shape[-1]
    mlp_blocks = lax.psum_scatter(
        jnp.concatenate(
            [
                rows_product(residual_flat, grad_gate_flat),
                rows_product(residual_flat, grad_up_flat),
                rows_product(grad_ff_flat, hidden_flat),
            ],
            axis=1,
        ).astype(jnp.bfloat16),
        "dp",
        scatter_dimension=0,
        tiled=True,
    ).astype(jnp.float32)
    grad_gate, grad_up, grad_down_rows = (
        lax.all_to_all(
            mlp_blocks[:, :block_width].astype(jnp.bfloat16),
            "seq",
            split_axis=0,
            concat_axis=1,
            tiled=True,
        ).astype(jnp.float32),
        lax.all_to_all(
            mlp_blocks[:, block_width : 2 * block_width].astype(jnp.bfloat16),
            "seq",
            split_axis=0,
            concat_axis=1,
            tiled=True,
        ).astype(jnp.float32),
        lax.all_to_all(
            mlp_blocks[:, 2 * block_width :].astype(jnp.bfloat16),
            "seq",
            split_axis=0,
            concat_axis=1,
            tiled=True,
        ).astype(jnp.float32),
    )
    grad_down = grad_down_rows.T
    grad_attn32, grad_attng = attn_back(grad_resid)
    grad_attn = grad_attn32.astype(jnp.bfloat16)
    grad_mixed = back_project(grad_attn, wo_all).astype(jnp.bfloat16)
    grad_mixed_heads = lax.all_to_all(grad_mixed, "seq", split_axis=2, concat_axis=1, tiled=True)
    grad_qh, grad_kh, grad_vh = attend_back(
        q_heads, k_heads, v_heads, grad_mixed_heads, log_totals, segments
    )
    grad_q_rot, grad_k_rot, grad_value_low = (
        lax.all_to_all(grad_qh, "seq", split_axis=1, concat_axis=2, tiled=True),
        lax.all_to_all(grad_kh, "seq", split_axis=1, concat_axis=2, tiled=True),
        lax.all_to_all(grad_vh, "seq", split_axis=1, concat_axis=2, tiled=True),
    )
    grad_q32, grad_qg = query_back(grad_q_rot.astype(jnp.float32))
    grad_k32, grad_kg = key_back(grad_k_rot.astype(jnp.float32))
    grad_query_low = grad_q32.astype(jnp.bfloat16)
    grad_key_low = grad_k32.astype(jnp.bfloat16)
    input_grad = (
        grad_resid
        + back_project(grad_query_low, wq_all)
        + back_project(grad_key_low, wk_all)
        + back_project(grad_value_low, wv_all)
    ).astype(jnp.bfloat16)
    input_flat = layer_input.reshape(-1, model_width)
    mixed_flat = mixed_local.reshape(-1, model_width)
    grad_query_flat = grad_query_low.reshape(-1, model_width)
    grad_key_flat = grad_key_low.reshape(-1, model_width)
    grad_value_flat = grad_value_low.reshape(-1, model_width)
    grad_attn_flat = grad_attn.reshape(-1, model_width)
    attn_part = lax.psum_scatter(
        jnp.concatenate(
            [
                rows_product(input_flat, grad_query_flat),
                rows_product(input_flat, grad_key_flat),
                rows_product(input_flat, grad_value_flat),
                rows_product(mixed_flat, grad_attn_flat),
            ],
            axis=1,
        ),
        ("dp", "seq"),
        scatter_dimension=0,
        tiled=True,
    )
    gain_stack = jnp.stack([grad_qg, grad_kg, grad_attng, grad_ffg])
    gain_shares = lax.psum_scatter(gain_stack, ("dp", "seq"), scatter_dimension=1, tiled=True)
    grad_query = attn_part[:, :model_width]
    grad_key = attn_part[:, model_width : 2 * model_width]
    grad_value = attn_part[:, 2 * model_width : 3 * model_width]
    grad_output = attn_part[:, 3 * model_width :]
    return (
        activation,
        input_grad,
        grad_query,
        grad_key,
        grad_value,
        grad_output,
        grad_gate,
        grad_up,
        grad_down,
        gain_shares[0],
        gain_shares[1],
        gain_shares[2],
        gain_shares[3],
    )


def solution(mesh):
    placed = (
        P("dp", "seq", None),
        P("dp", None),
        P(("dp", "seq"), None),
        P(("dp", "seq"), None),
        P(("dp", "seq"), None),
        P(("dp", "seq"), None),
        P(("dp", "seq"), None),
        P(("dp", "seq"), None),
        P(None, ("dp", "seq")),
        P(),
        P(),
        P(),
        P(),
        P("dp", "seq", None),
    )
    return jax.shard_map(
        shards,
        mesh=mesh,
        in_specs=placed,
        out_specs=(
            P("dp", "seq", None),
            P("dp", "seq", None),
            P(("dp", "seq"), None),
            P(("dp", "seq"), None),
            P(("dp", "seq"), None),
            P(("dp", "seq"), None),
            P(("dp", "seq"), None),
            P(("dp", "seq"), None),
            P(None, ("dp", "seq")),
            P(("dp", "seq")),
            P(("dp", "seq")),
            P(("dp", "seq")),
            P(("dp", "seq")),
        ),
        check_vma=False,
    )
```

profile of v0, /device:TPU:0, one launch (start us, length us, event | category | flops | bytes accessed | tf_op | source)
XLA Modules:
  0.0 3019.1 jit_solution(3999838460059790055)
XLA Ops:
  19.4 30.5 %all-to-all-done.4 = bf16[64,4,2048]{2,0,1:T(8,128)(2,1)S(1)} async-done(((bf16[64,4,2048]{2,0,1:T(8,128)(2,1)}), bf16[64,4,2048]{2,0,1:T(8,128)(2,1)S(1)}, u32[]{:S(2)}, u32[]{:S(2)}) %all-to-all-start.4) | async-done | bytes 1048608 | tf_op jit(solution)/shard_map/all_to_all | solution.py:216
  50.9 51.7 %all-gather.14.cloned.1.call-done = bf16[2048,2048]{1,0:T(8,128)(2,1)} async-done(((bf16[64,2048]{1,0:T(8,128)(2,1)}), bf16[2048,2048]{1,0:T(8,128)(2,1)}) %all-gather.14.cloned.1.call-update) | async-done | bytes 8388624 | tf_op jit(solution)/shard_map/all_gather | solution.py:192
  134.0 58.4 %all-gather.12.cloned.1.call-done = bf16[2048,2048]{1,0:T(8,128)(2,1)} async-done(((bf16[64,2048]{1,0:T(8,128)(2,1)}), bf16[2048,2048]{1,0:T(8,128)(2,1)}) %all-gather.12.cloned.1.call-update) | async-done | bytes 8388624 | tf_op jit(solution)/shard_map/all_gather | solution.py:191
  201.6 69.9 %all-gather.10.cloned.1.call-done = bf16[2048,2048]{1,0:T(8,128)(2,1)} async-done(((bf16[64,2048]{1,0:T(8,128)(2,1)}), bf16[2048,2048]{1,0:T(8,128)(2,1)}) %all-gather.10.cloned.1.call-update) | async-done | bytes 8388624 | tf_op jit(solution)/shard_map/all_gather | solution.py:190
  325.9 32.2 %all-to-all-done.1 = bf16[4,2,65536]{2,1,0:T(2,128)(2,1)} async-done(((bf16[4,2,65536]{2,1,0:T(2,128)(2,1)}), bf16[4,2,65536]{2,1,0:T(2,128)(2,1)}, u32[]{:S(2)}, u32[]{:S(2)}) %all-to-all-start.1) | async-done | bytes 1048608 | tf_op jit(solution)/shard_map/all_to_all | solution.py:205
  372.0 15.0 all-to-all-done
  399.5 25.0 while.27
  444.4 28.9 all_to_all.204
  485.9 55.2 %all_to_all.205 = bf16[64,4,2048]{2,0,1:T(8,128)(2,1)} all-to-all(bf16[64,4,2048]{2,0,1:T(8,128)(2,1)S(1)} %bitcast.443), channel_id=1, replica_groups=mesh['dp'=8,'seq'=4] {'seq'}, dimensions={1} | all-to-all | bytes 2097152 | tf_op jit(solution)/shard_map/all_to_all | solution.py:217
  541.3 52.8 %all_to_all.206 = bf16[64,4,2048]{2,0,1:T(8,128)(2,1)} all-to-all(bf16[64,4,2048]{2,0,1:T(8,128)(2,1)S(1)} %bitcast.444), channel_id=1, replica_groups=mesh['dp'=8,'seq'=4] {'seq'}, dimensions={1} | all-to-all | bytes 2097152 | tf_op jit(solution)/shard_map/all_to_all | solution.py:218
  604.0 14.7 fusion.49
  618.7 39.7 %all-gather.22.cloned.1.call-done = bf16[2048,2048]{1,0:T(8,128)(2,1)} async-done(((bf16[256,2048]{1,0:T(8,128)(2,1)}), bf16[2048,2048]{1,0:T(8,128)(2,1)}) %all-gather.22.cloned.1.call-update) | async-done | bytes 8388624 | tf_op jit(solution)/shard_map/all_gather | solution.py:222
  658.4 17.0 multiply_convert_fusion.2
  675.4 39.3 %all-gather.24.cloned.1.call-done = bf16[2048,2048]{1,0:T(8,128)(2,1)} async-done(((bf16[256,2048]{1,0:T(8,128)(2,1)}), bf16[2048,2048]{1,0:T(8,128)(2,1)}) %all-gather.24.cloned.1.call-update) | async-done | bytes 8388624 | tf_op jit(solution)/shard_map/all_gather | solution.py:223
  714.8 14.0 convert_bitcast_fusion
  728.8 68.3 %all-gather.26.cloned.1.call-done = bf16[1,1024,2048]{2,1,0:T(8,128)(2,1)} async-done(((bf16[1,256,2048]{2,1,0:T(8,128)(2,1)}), bf16[1,1024,2048]{2,1,0:T(8,128)(2,1)}) %all-gather.26.cloned.1.call-update) | async-done | bytes 4194320 | tf_op jit(solution)/shard_map/all_gather | solution.py:227
  797.1 155.8 %all-reduce.6.cloned.1.call-done = bf16[1,1024,2048]{2,1,0:T(8,128)(2,1)} async-done(((bf16[1,1024,2048]{2,1,0:T(8,128)(2,1)}), bf16[1,1024,2048]{2,1,0:T(8,128)(2,1)}) %all-reduce.6.cloned.1.call-update) | async-done | bytes 4194320 | tf_op jit(solution)/shard_map/psum | solution.py:232
  958.0 23.0 multiply_convert_fusion.1
  993.7 13.8 add_bitcast_fusion
  1007.5 14.5 convolution_convert_fusion.1
  1033.3 13.6 convolution_convert_fusion
  1046.9 18.1 pad_maximum_fusion.1
  1072.3 78.8 %reduce-scatter.9.cloned.1.call-done = f32[1,256,2048]{2,1,0:T(8,128)} async-done(((f32[1,1024,2048]{2,1,0:T(8,128)}), f32[1,256,2048]{2,1,0:T(8,128)}) %reduce-scatter.9.cloned.1.call-update) | async-done | bytes 2097168 | tf_op jit(solution)/shard_map/reduce_scatter | solution.py:248
  1184.4 25.7 all-to-all-done.7
  1221.0 43.4 %while.28 = (s32[]{:T(128)}, f32[1,1024,4,128]{1,3,2,0:T(8,128)S(1)}, f32[1,1024,4,128]{1,3,2,0:T(8,128)}, bf16[2,1,512,4,128]{4,3,2,0,1:T(4,128)(2,1)}, s32[2]{...) while((s32[]{:T(128)}, ...), condition=%wide.region_15.16_spmd.clone, body=%wide.region_13.15_spmd.clone.sunk | while | flops 2720528896 | bytes 98113936 | solution.py:150
  1297.3 14.4 all-to-all-done.8
  1420.9 45.1 %pad_maximum_fusion = f32[2048,8192]{0,1:T(8,128)} fusion(f32[2048,2048]{0,1:T(8,128)} %fusion.92, f32[2048,2048]{0,1:T(8,128)} %convolution_bitcast_fusion, f32[2048,2048]{0,1:T(8,128)} %convolution_bitcast_fusion.1, f32[2048,2048]{0,1:T(8,128)} %convolution_bitcast_fusion.2), kind=kLoop, calls=%fused_computation.57 | loop fusion | flops 50331648 | bytes 134217728 | tf_op jit(solution)/shard_map/concatenate | solution.py:321
  1466.0 61.3 %copy.230 = f32[2048,8192]{1,0:T(8,128)} copy(f32[2048,8192]{0,1:T(8,128)} %pad_maximum_fusion) | data formatting | bytes 134217728
  1539.3 24.2 all-to-all-done.13
  1584.8 37.2 %all-to-all-done.12 = bf16[4,64,2048]{2,1,0:T(8,128)(2,1)} async-done(((bf16[4,64,2048]{2,1,0:T(8,128)(2,1)}), bf16[4,64,2048]{2,1,0:T(8,128)(2,1)}, u32[]{:S(2)}, u32[]{:S(2)}) %all-to-all-start.12) | async-done | bytes 1048608 | tf_op jit(solution)/shard_map/all_to_all | solution.py:276
  1643.8 37.9 %all-to-all-done.11 = bf16[4,64,2048]{2,1,0:T(8,128)(2,1)} async-done(((bf16[4,64,2048]{2,1,0:T(8,128)(2,1)}), bf16[4,64,2048]{2,1,0:T(8,128)(2,1)}, u32[]{:S(2)}, u32[]{:S(2)}) %all-to-all-start.11) | async-done | bytes 1048608 | tf_op jit(solution)/shard_map/all_to_all | solution.py:269
  1684.6 1324.6 %reduce-scatter.13.cloned.1.call-done = f32[64,8192]{1,0:T(8,128)} async-done(((f32[2048,8192]{1,0:T(8,128)}), f32[64,8192]{1,0:T(8,128)}) %reduce-scatter.13.cloned.1.call-update) | async-done | bytes 2097168
  (399 shorter events, 517.1 us)
Async XLA Ops:
  7.2 95.5 %copy-start.13 = (bf16[1,256,2048]{2,1,0:T(8,128)(2,1)S(1)}, bf16[1,256,2048]{2,1,0:T(8,128)(2,1)}, u32[]{:S(2)}) copy-start(bf16[1,256,2048]{2,1,0:T(8,128)(2,1)} %param.18) | copy-start | bytes 3145732
  7.2 95.5 %all-gather.14.cloned.1.call-start = ((), (), s32[]{:S(2)}) async-start(), calls=%async_computation.20 | async-start | bytes 8650752 | tf_op jit(solution)/shard_map/all_gather | solution.py:192
  7.9 184.5 %all-gather.12.cloned.1.call-start = ((), (), s32[]{:S(2)}) async-start(), calls=%async_computation.19 | async-start | bytes 8650752 | tf_op jit(solution)/shard_map/all_gather | solution.py:191
  8.7 262.8 %all-gather.10.cloned.1.call-start = ((), (), s32[]{:S(2)}) async-start(), calls=%async_computation.18 | async-start | bytes 8650752 | tf_op jit(solution)/shard_map/all_gather | solution.py:190
  9.4 467.4 %all-gather.16.cloned.1.call-start = ((), (), s32[]{:S(2)}) async-start(), calls=%async_computation.21 | async-start | bytes 8650752 | tf_op jit(solution)/shard_map/all_gather | solution.py:193
  12.3 37.6 %all-to-all-start.4 = ((bf16[64,4,2048]{2,0,1:T(8,128)(2,1)}), bf16[64,4,2048]{2,0,1:T(8,128)(2,1)S(1)}, u32[]{:S(2)}, u32[]{:S(2)}) async-start(bf16[64,4,2048]{2,0,1:T(8,128)(2,1)} %bitcast.345), calls=%async_computation.4 | async-start | bytes 2097152 | tf_op jit(solution)/shard_map/all_to_all | solution.py:216
  18.6 576.3 %all-gather.20.cloned.1.call-start = ((), (), s32[]{:S(2)}) async-start(), calls=%async_computation.23 | async-start | bytes 9437184 | tf_op jit(solution)/shard_map/all_gather | solution.py:221
  129.5 178.2 %all-to-all-start.2 = ((bf16[4,2,65536]{2,1,0:T(2,128)(2,1)}), bf16[4,2,65536]{2,1,0:T(2,128)(2,1)}, u32[]{:S(2)}, u32[]{:S(2)}) async-start(bf16[4,2,65536]{2,1,0:T(2,128)(2,1)} %reshape.886), calls=%async_computation.2 | async-start | bytes 2097152 | tf_op jit(solution)/shard_map/all_to_all | solution.py:206
  307.7 50.4 %all-to-all-start.1 = ((bf16[4,2,65536]{2,1,0:T(2,128)(2,1)}), bf16[4,2,65536]{2,1,0:T(2,128)(2,1)}, u32[]{:S(2)}, u32[]{:S(2)}) async-start(bf16[4,2,65536]{2,1,0:T(2,128)(2,1)} %reshape.884), calls=%async_computation.1 | async-start | bytes 2097152 | tf_op jit(solution)/shard_map/all_to_all | solution.py:205
  358.1 28.9 all-to-all-start
  362.4 241.6 %all-gather.18.cloned.1.call-start = ((), (), s32[]{:S(2)}) async-start(), calls=%async_computation.22 | async-start | bytes 5242880 | tf_op jit(solution)/shard_map/all_gather | solution.py:226
  485.7 172.7 %all-gather.22.cloned.1.call-start = ((), (), s32[]{:S(2)}) async-start(), calls=%async_computation.24 | async-start | bytes 9437184 | tf_op jit(solution)/shard_map/all_gather | solution.py:222
  541.1 173.7 %all-gather.24.cloned.1.call-start = ((), (), s32[]{:S(2)}) async-start(), calls=%async_computation.25 | async-start | bytes 9437184 | tf_op jit(solution)/shard_map/all_gather | solution.py:223
  594.1 203.0 %all-gather.26.cloned.1.call-start = ((), (), s32[]{:S(2)}) async-start(), calls=%async_computation.27 | async-start | bytes 5242880 | tf_op jit(solution)/shard_map/all_gather | solution.py:227
  594.8 358.1 %all-reduce.6.cloned.1.call-start = ((), (), s32[]{:S(2)}) async-start(), calls=%async_computation.26 | async-start | bytes 8388608 | tf_op jit(solution)/shard_map/psum | solution.py:232
  728.7 224.2 %copy-start.60 = (f32[2048]{0:T(1024)S(1)}, f32[2048]{0:T(1024)}, u32[]{:S(2)}) copy-start(f32[2048]{0:T(1024)} %param.30) | copy-start | bytes 24580
  728.8 422.3 %reduce-scatter.9.cloned.1.call-start = ((), (), s32[]{:S(2)}) async-start(), calls=%async_computation.28 | async-start | bytes 10485760 | tf_op jit(solution)/shard_map/reduce_scatter | solution.py:248
  1007.5 519.9 %reduce-scatter.11.cloned.1.call-start = ((), (), s32[]{:S(2)}) async-start(), calls=%async_computation.29 | async-start | bytes 28311552 | tf_op jit(solution)/shard_map/reduce_scatter | solution.py:255
  1065.0 86.1 %copy-start.12 = (f32[256,2048]{1,0:T(8,128)S(1)}, f32[256,2048]{1,0:T(8,128)}, u32[]{:S(2)}) copy-start(f32[256,2048]{1,0:T(8,128)} %copy-done.11) | copy-start | bytes 6291460
  1065.0 86.1 %copy-start.15 = (bf16[1,256,2048]{2,1,0:T(8,128)(2,1)S(1)}, bf16[1,256,2048]{2,1,0:T(8,128)(2,1)}, u32[]{:S(2)}) copy-start(bf16[1,256,2048]{2,1,0:T(8,128)(2,1)} %param.18) | copy-start | bytes 3145732
  1065.0 86.1 %copy-start.51 = (f32[2048]{0:T(1024)S(1)}, f32[2048]{0:T(1024)}, u32[]{:S(2)}) copy-start(f32[2048]{0:T(1024)} %param.29) | copy-start | bytes 24580
  1065.0 86.1 %copy-start.66 = (f32[256]{0:T(256)S(1)}, f32[256]{0:T(256)}, u32[]{:S(2)}) copy-start(f32[256]{0:T(256)} %copy-done.65) | copy-start | bytes 3076
  1072.3 85.2 %copy-start.68 = (f32[256]{0:T(256)S(1)}, f32[256]{0:T(256)}, u32[]{:S(2)}) copy-start(f32[256]{0:T(256)} %copy-done.67) | copy-start | bytes 3076
  1180.0 30.2 %all-to-all-start.7 = ((bf16[4,2,65536]{2,1,0:T(2,128)(2,1)}), bf16[4,2,65536]{2,1,0:T(2,128)(2,1)S(1)}, u32[]{:S(2)}, u32[]{:S(2)}) async-start(bf16[4,2,65536]{2,1,0:T(2,128)(2,1)} %reshape.890), calls=%async_computation.8 | async-start | bytes 2097152 | tf_op jit(solution)/shard_map/all_to_all | solution.py:295
  1281.5 30.1 all-to-all-start.8
  1311.7 29.7 all-to-all-start.9
  1341.4 28.7 all-to-all-start.10
  1344.9 289.8 %reduce-scatter.15.cloned.1.call-start = ((), (), s32[]{:S(2)}) async-start(), calls=%async_computation.31 | async-start | bytes 1081344
  1420.9 1588.4 %reduce-scatter.13.cloned.1.call-start = ((), (), s32[]{:S(2)}) async-start(), calls=%async_computation.30 | async-start | bytes 69206016
  1532.2 31.3 %all-to-all-start.13 = ((bf16[4,64,2048]{2,1,0:T(8,128)(2,1)}), bf16[4,64,2048]{2,1,0:T(8,128)(2,1)S(1)}, u32[]{:S(2)}, u32[]{:S(2)}) async-start(bf16[4,64,2048]{2,1,0:T(8,128)(2,1)} %bitcast.442), calls=%async_computation.15 | async-start | bytes 2097152 | tf_op jit(solution)/shard_map/all_to_all | solution.py:283
  1563.5 58.4 %all-to-all-start.12 = ((bf16[4,64,2048]{2,1,0:T(8,128)(2,1)}), bf16[4,64,2048]{2,1,0:T(8,128)(2,1)}, u32[]{:S(2)}, u32[]{:S(2)}) async-start(bf16[4,64,2048]{2,1,0:T(8,128)(2,1)} %bitcast.441), calls=%async_computation.14 | async-start | bytes 2097152 | tf_op jit(solution)/shard_map/all_to_all | solution.py:276
  1622.0 59.8 %all-to-all-start.11 = ((bf16[4,64,2048]{2,1,0:T(8,128)(2,1)}), bf16[4,64,2048]{2,1,0:T(8,128)(2,1)}, u32[]{:S(2)}, u32[]{:S(2)}) async-start(bf16[4,64,2048]{2,1,0:T(8,128)(2,1)} %bitcast.438), calls=%async_computation.13 | async-start | bytes 2097152 | tf_op jit(solution)/shard_map/all_to_all | solution.py:269
  (76 other events, 1037.8 us)
Sparse Core Ops, SparseCore 0:
  11.0 91.6 all-gather.13
  105.6 86.8 all-gather.11
  195.4 76.0 all-gather.9
  274.3 89.3 all-gather.15
  365.4 52.4 all-gather.19
  485.8 118.1 all-gather.17
  605.9 52.5 all-gather.21
  660.3 54.3 all-gather.23
  716.3 80.7 all-gather.25
  799.3 153.5 all-reduce.5
  1007.6 143.4 reduce-scatter.8
  1155.0 157.5 reduce-scatter.10
  1421.0 137.4 reduce-scatter.14
  1560.7 1448.5 reduce-scatter.12
where the time goes:
time: 3030 us; the launch traced here: 3020 us
  waiting for transfers between devices  2130 us (70%)
  matrix products  256 us (8%)
  local copies, waits for them, and re-layouts  223 us (7%)
  other arithmetic  199 us (7%)
  blocking collectives  137 us (5%)
  starting transfers between devices  50.6 us (2%)
    unnamed x16, waiting for transfers between devices  1330 us
    psum x1, waiting for transfers between devices, shards(): lax.psum(back_project(hidden_low, wd_blk).astype(jnp.bfloat16), 'seq')  156 us
    unnamed x173, local copies, waits for them, and re-layouts  131 us
    unnamed x15, other arithmetic  81.6 us
    dot_general x7, matrix products, project(): return jnp.dot(left, weight, preferred_element_type=jnp.float32)  79.2 us
    reduce_scatter x1, waiting for transfers between devices, shards(): lax.psum_scatter(partial_resid, 'seq', scatter_dimension=1, tiled=True)  78.8 us
    dot_general x7, matrix products, rows_product(): lax.dot_general(left, right, (((0,), (0,)), ((), ())), preferred_element_...  71.9 us
    dot_general x7, matrix products, back_project(): lax.dot_general(grad_in, weight, (((grad_in.ndim - 1,), (1,)), ((), ())),...  69.9 us
  transfers between devices with their start and end apart: 25, of which 20 were waited for; matrix products, arithmetic and copies ran while one was open for 20% of the time, Pallas kernels for 0%

commit v1 on v0

--- a/solution.py
+++ b/solution.py
@@ -229,9 +229,8 @@
     gate_act = project(resid_full, wg_blk)
     up_act = project(resid_full, wu_blk)
     hidden_low = silu_mix(gate_act, up_act).astype(jnp.bfloat16)
-    ff_full = lax.psum(back_project(hidden_low, wd_blk).astype(jnp.bfloat16), "seq").astype(
-        jnp.float32
-    )
+    turn_leaves = lambda row_data: jnp.sum(jax.lax.all_gather(row_data, "seq"), axis=0)
+    ff_full = turn_leaves(back_project(hidden_low, wd_blk).astype(jnp.bfloat16)).astype(jnp.float32)
     ff_own = lax.dynamic_slice_in_dim(ff_full, offset, local_len, 1)
     ff_normed, ff_back = jax.vjp(rms_norm, ff_own, ff_gain)
     activation = (residual + ff_normed).astype(jnp.bfloat16)

time: 3030 us -> 3170 us (1.046)
  waiting for transfers between devices: 2130 us -> 2250 us
    all_gather x0 -> x1, waiting for transfers between devices: none -> 286 us  [shards(): jax.lax.all_gather(row_data, 'seq')]
    psum x1 -> x0, waiting for transfers between devices: 156 us -> none  [shards(): lax.psum(back_project(hidden_low, wd_blk).astype(jnp.bfloat16), 'seq')]
  transfers between devices with their start and end apart: 25 -> 25, of which waited for: 20 -> 20; matrix products, arithmetic and copies ran while one was open for 20% -> 19% of each run, Pallas kernels for 0% -> 0%
where the time goes in v1:
time: 3170 us; the launch traced here: 3160 us
  waiting for transfers between devices  2250 us (71%)
  matrix products  257 us (8%)
  local copies, waits for them, and re-layouts  223 us (7%)
  other arithmetic  215 us (7%)
  blocking collectives  137 us (4%)
  starting transfers between devices  50.9 us (2%)
    unnamed x16, waiting for transfers between devices  1330 us
    all_gather x1, waiting for transfers between devices, shards(): jax.lax.all_gather(row_data, 'seq')  286 us
    unnamed x173, local copies, waits for them, and re-layouts  131 us
    unnamed x15, other arithmetic  81.6 us
    dot_general x7, matrix products, project(): return jnp.dot(left, weight, preferred_element_type=jnp.float32)  78.9 us
    reduce_scatter x1, waiting for transfers between devices, shards(): lax.psum_scatter(partial_resid, 'seq', scatter_dimension=1, tiled=True)  78.4 us
    dot_general x7, matrix products, rows_product(): lax.dot_general(left, right, (((0,), (0,)), ((), ())), preferred_element_...  71.8 us
    dot_general x7, matrix products, back_project(): lax.dot_general(grad_in, weight, (((grad_in.ndim - 1,), (1,)), ((), ())),...  70.4 us
  transfers between devices with their start and end apart: 25, of which 20 were waited for; matrix products, arithmetic and copies ran while one was open for 19% of the time, Pallas kernels for 0%

profile of v1, /device:TPU:0, one launch (start us, length us, event | category | flops | bytes accessed | tf_op | source)
XLA Modules:
  0.0 3162.6 jit_solution(10102721231775856310)
XLA Ops:
  19.4 30.5 all-to-all-done.4
  51.0 51.7 %all-gather.16.cloned.1.call-done = bf16[2048,2048]{1,0:T(8,128)(2,1)} async-done(((bf16[64,2048]{1,0:T(8,128)(2,1)}), bf16[2048,2048]{1,0:T(8,128)(2,1)}) %all-gather.16.cloned.1.call-update) | async-done | bytes 8388624 | tf_op jit(solution)/shard_map/all_gather | solution.py:192
  134.0 58.4 %all-gather.14.cloned.1.call-done = bf16[2048,2048]{1,0:T(8,128)(2,1)} async-done(((bf16[64,2048]{1,0:T(8,128)(2,1)}), bf16[2048,2048]{1,0:T(8,128)(2,1)}) %all-gather.14.cloned.1.call-update) | async-done | bytes 8388624 | tf_op jit(solution)/shard_map/all_gather | solution.py:191
  201.6 69.9 %all-gather.12.cloned.1.call-done = bf16[2048,2048]{1,0:T(8,128)(2,1)} async-done(((bf16[64,2048]{1,0:T(8,128)(2,1)}), bf16[2048,2048]{1,0:T(8,128)(2,1)}) %all-gather.12.cloned.1.call-update) | async-done | bytes 8388624 | tf_op jit(solution)/shard_map/all_gather | solution.py:190
  325.9 32.3 %all-to-all-done.1 = bf16[4,2,65536]{2,1,0:T(2,128)(2,1)} async-done(((bf16[4,2,65536]{2,1,0:T(2,128)(2,1)}), bf16[4,2,65536]{2,1,0:T(2,128)(2,1)}, u32[]{:S(2)}, u32[]{:S(2)}) %all-to-all-start.1) | async-done | bytes 1048608 | tf_op jit(solution)/shard_map/all_to_all | solution.py:205
  372.1 14.9 all-to-all-done
  399.5 25.0 while.27
  444.4 28.8 all_to_all.204
  485.8 55.2 %all_to_all.205 = bf16[64,4,2048]{2,0,1:T(8,128)(2,1)} all-to-all(bf16[64,4,2048]{2,0,1:T(8,128)(2,1)S(1)} %bitcast.465), channel_id=1, replica_groups=mesh['dp'=8,'seq'=4] {'seq'}, dimensions={1} | all-to-all | bytes 2097152 | tf_op jit(solution)/shard_map/all_to_all | solution.py:217
  541.2 52.8 %all_to_all.206 = bf16[64,4,2048]{2,0,1:T(8,128)(2,1)} all-to-all(bf16[64,4,2048]{2,0,1:T(8,128)(2,1)S(1)} %bitcast.466), channel_id=1, replica_groups=mesh['dp'=8,'seq'=4] {'seq'}, dimensions={1} | all-to-all | bytes 2097152 | tf_op jit(solution)/shard_map/all_to_all | solution.py:218
  604.0 14.6 fusion.50
  618.5 39.9 %all-gather.24.cloned.1.call-done = bf16[2048,2048]{1,0:T(8,128)(2,1)} async-done(((bf16[256,2048]{1,0:T(8,128)(2,1)}), bf16[2048,2048]{1,0:T(8,128)(2,1)}) %all-gather.24.cloned.1.call-update) | async-done | bytes 8388624 | tf_op jit(solution)/shard_map/all_gather | solution.py:222
  658.4 16.9 multiply_convert_fusion.2
  675.3 39.4 %all-gather.26.cloned.1.call-done = bf16[2048,2048]{1,0:T(8,128)(2,1)} async-done(((bf16[256,2048]{1,0:T(8,128)(2,1)}), bf16[2048,2048]{1,0:T(8,128)(2,1)}) %all-gather.26.cloned.1.call-update) | async-done | bytes 8388624 | tf_op jit(solution)/shard_map/all_gather | solution.py:223
  714.8 13.9 convolution_convert_fusion.3
  729.3 286.3 %all-gather.30.cloned.1.call-done = bf16[4096,2048]{1,0:T(8,128)(2,1)} async-done(((bf16[1024,2048]{1,0:T(8,128)(2,1)}), bf16[4096,2048]{1,0:T(8,128)(2,1)}) %all-gather.30.cloned.1.call-update) | async-done | bytes 16777232 | tf_op jit(solution)/shard_map/all_gather | solution.py:232
  1031.6 64.4 %all-gather.28.cloned.1.call-done = bf16[1,1024,2048]{2,1,0:T(8,128)(2,1)} async-done(((bf16[1,256,2048]{2,1,0:T(8,128)(2,1)}), bf16[1,1024,2048]{2,1,0:T(8,128)(2,1)}) %all-gather.28.cloned.1.call-update) | async-done | bytes 4194320 | tf_op jit(solution)/shard_map/all_gather | solution.py:227
  1101.1 23.0 multiply_convert_fusion.1
  1136.8 13.6 add_bitcast_fusion
  1150.5 14.5 convolution_convert_fusion.1
  1176.2 13.5 convolution_convert_fusion
  1189.8 18.1 pad_maximum_fusion.1
  1215.2 78.4 %reduce-scatter.9.cloned.1.call-done = f32[1,256,2048]{2,1,0:T(8,128)} async-done(((f32[1,1024,2048]{2,1,0:T(8,128)}), f32[1,256,2048]{2,1,0:T(8,128)}) %reduce-scatter.9.cloned.1.call-update) | async-done | bytes 2097168 | tf_op jit(solution)/shard_map/reduce_scatter | solution.py:247
  1327.3 25.4 all-to-all-done.7
  1363.5 43.5 %while.28 = (s32[]{:T(128)}, f32[1,1024,4,128]{1,3,2,0:T(8,128)S(1)}, f32[1,1024,4,128]{1,3,2,0:T(8,128)}, bf16[2,1,512,4,128]{4,3,2,0,1:T(4,128)(2,1)}, s32[2]{...) while((s32[]{:T(128)}, ...), condition=%wide.region_15.16_spmd.clone, body=%wide.region_13.15_spmd.clone.sunk | while | flops 2720528896 | bytes 98113936 | solution.py:150
  1439.9 14.2 all-to-all-done.8
  1563.3 45.0 %pad_maximum_fusion = f32[2048,8192]{0,1:T(8,128)} fusion(f32[2048,2048]{0,1:T(8,128)} %fusion.94, f32[2048,2048]{0,1:T(8,128)} %convolution_bitcast_fusion, f32[2048,2048]{0,1:T(8,128)} %convolution_bitcast_fusion.1, f32[2048,2048]{0,1:T(8,128)} %convolution_bitcast_fusion.2), kind=kLoop, calls=%fused_computation.57 | loop fusion | flops 50331648 | bytes 134217728 | tf_op jit(solution)/shard_map/concatenate | solution.py:320
  1608.3 61.2 %copy.230 = f32[2048,8192]{1,0:T(8,128)} copy(f32[2048,8192]{0,1:T(8,128)} %pad_maximum_fusion) | data formatting | bytes 134217728
  1681.5 24.2 all-to-all-done.13
  1727.6 36.1 %all-to-all-done.12 = bf16[4,64,2048]{2,1,0:T(8,128)(2,1)} async-done(((bf16[4,64,2048]{2,1,0:T(8,128)(2,1)}), bf16[4,64,2048]{2,1,0:T(8,128)(2,1)}, u32[]{:S(2)}, u32[]{:S(2)}) %all-to-all-start.12) | async-done | bytes 1048608 | tf_op jit(solution)/shard_map/all_to_all | solution.py:275
  1785.6 34.6 %all-to-all-done.11 = bf16[4,64,2048]{2,1,0:T(8,128)(2,1)} async-done(((bf16[4,64,2048]{2,1,0:T(8,128)(2,1)}), bf16[4,64,2048]{2,1,0:T(8,128)(2,1)}, u32[]{:S(2)}, u32[]{:S(2)}) %all-to-all-start.11) | async-done | bytes 1048608 | tf_op jit(solution)/shard_map/all_to_all | solution.py:268
  1823.1 1329.7 %reduce-scatter.13.cloned.1.call-done = f32[64,8192]{1,0:T(8,128)} async-done(((f32[2048,8192]{1,0:T(8,128)}), f32[64,8192]{1,0:T(8,128)}) %reduce-scatter.13.cloned.1.call-update) | async-done | bytes 2097168
  (401 shorter events, 534.8 us)
Async XLA Ops:
  7.2 95.5 %copy-start.15 = (bf16[1,256,2048]{2,1,0:T(8,128)(2,1)S(1)}, bf16[1,256,2048]{2,1,0:T(8,128)(2,1)}, u32[]{:S(2)}) copy-start(bf16[1,256,2048]{2,1,0:T(8,128)(2,1)} %param.18) | copy-start | bytes 3145732
  7.2 95.5 %all-gather.16.cloned.1.call-start = ((), (), s32[]{:S(2)}) async-start(), calls=%async_computation.20 | async-start | bytes 8650752 | tf_op jit(solution)/shard_map/all_gather | solution.py:192
  7.9 184.5 %all-gather.14.cloned.1.call-start = ((), (), s32[]{:S(2)}) async-start(), calls=%async_computation.19 | async-start | bytes 8650752 | tf_op jit(solution)/shard_map/all_gather | solution.py:191
  8.7 262.8 %all-gather.12.cloned.1.call-start = ((), (), s32[]{:S(2)}) async-start(), calls=%async_computation.18 | async-start | bytes 8650752 | tf_op jit(solution)/shard_map/all_gather | solution.py:190
  9.4 467.3 %all-gather.18.cloned.1.call-start = ((), (), s32[]{:S(2)}) async-start(), calls=%async_computation.21 | async-start | bytes 8650752 | tf_op jit(solution)/shard_map/all_gather | solution.py:193
  12.3 37.6 %all-to-all-start.4 = ((bf16[64,4,2048]{2,0,1:T(8,128)(2,1)}), bf16[64,4,2048]{2,0,1:T(8,128)(2,1)S(1)}, u32[]{:S(2)}, u32[]{:S(2)}) async-start(bf16[64,4,2048]{2,0,1:T(8,128)(2,1)} %bitcast.366), calls=%async_computation.4 | async-start | bytes 2097152 | tf_op jit(solution)/shard_map/all_to_all | solution.py:216
  18.6 575.5 %all-gather.22.cloned.1.call-start = ((), (), s32[]{:S(2)}) async-start(), calls=%async_computation.23 | async-start | bytes 9437184 | tf_op jit(solution)/shard_map/all_gather | solution.py:221
  129.5 178.2 %all-to-all-start.2 = ((bf16[4,2,65536]{2,1,0:T(2,128)(2,1)}), bf16[4,2,65536]{2,1,0:T(2,128)(2,1)}, u32[]{:S(2)}, u32[]{:S(2)}) async-start(bf16[4,2,65536]{2,1,0:T(2,128)(2,1)} %reshape.926), calls=%async_computation.2 | async-start | bytes 2097152 | tf_op jit(solution)/shard_map/all_to_all | solution.py:206
  198.2 84.3 %copy-start.8 = (f32[256,2048]{1,0:T(8,128)}, f32[256,2048]{1,0:T(8,128)S(1)}, u32[]{:S(2)}) copy-start(f32[256,2048]{1,0:T(8,128)S(1)} %get-tuple-element.411) | copy-start | bytes 6291460
  307.7 50.5 %all-to-all-start.1 = ((bf16[4,2,65536]{2,1,0:T(2,128)(2,1)}), bf16[4,2,65536]{2,1,0:T(2,128)(2,1)}, u32[]{:S(2)}, u32[]{:S(2)}) async-start(bf16[4,2,65536]{2,1,0:T(2,128)(2,1)} %reshape.924), calls=%async_computation.1 | async-start | bytes 2097152 | tf_op jit(solution)/shard_map/all_to_all | solution.py:205
  358.1 28.8 all-to-all-start
  362.4 241.5 %all-gather.20.cloned.1.call-start = ((), (), s32[]{:S(2)}) async-start(), calls=%async_computation.22 | async-start | bytes 5242880 | tf_op jit(solution)/shard_map/all_gather | solution.py:226
  485.7 172.8 %all-gather.24.cloned.1.call-start = ((), (), s32[]{:S(2)}) async-start(), calls=%async_computation.24 | async-start | bytes 9437184 | tf_op jit(solution)/shard_map/all_gather | solution.py:222
  541.1 173.7 %all-gather.26.cloned.1.call-start = ((), (), s32[]{:S(2)}) async-start(), calls=%async_computation.25 | async-start | bytes 9437184 | tf_op jit(solution)/shard_map/all_gather | solution.py:223
  594.0 421.6 %all-gather.30.cloned.1.call-start = ((), (), s32[]{:S(2)}) async-start(), calls=%async_computation.29 | async-start | bytes 20971520 | tf_op jit(solution)/shard_map/all_gather | solution.py:232
  728.7 367.3 %all-gather.28.cloned.1.call-start = ((), (), s32[]{:S(2)}) async-start(), calls=%async_computation.26 | async-start | bytes 5242880 | tf_op jit(solution)/shard_map/all_gather | solution.py:227
  729.3 564.3 %reduce-scatter.9.cloned.1.call-start = ((), (), s32[]{:S(2)}) async-start(), calls=%async_computation.27 | async-start | bytes 10485760 | tf_op jit(solution)/shard_map/reduce_scatter | solution.py:247
  1150.4 519.1 %reduce-scatter.11.cloned.1.call-start = ((), (), s32[]{:S(2)}) async-start(), calls=%async_computation.28 | async-start | bytes 28311552 | tf_op jit(solution)/shard_map/reduce_scatter | solution.py:254
  1207.9 85.7 %copy-start.14 = (f32[256,2048]{1,0:T(8,128)S(1)}, f32[256,2048]{1,0:T(8,128)}, u32[]{:S(2)}) copy-start(f32[256,2048]{1,0:T(8,128)} %copy-done.13) | copy-start | bytes 6291460
  1207.9 85.7 %copy-start.17 = (bf16[1,256,2048]{2,1,0:T(8,128)(2,1)S(1)}, bf16[1,256,2048]{2,1,0:T(8,128)(2,1)}, u32[]{:S(2)}) copy-start(bf16[1,256,2048]{2,1,0:T(8,128)(2,1)} %param.18) | copy-start | bytes 3145732
  1207.9 85.7 %copy-start.51 = (f32[2048]{0:T(1024)S(1)}, f32[2048]{0:T(1024)}, u32[]{:S(2)}) copy-start(f32[2048]{0:T(1024)} %param.29) | copy-start | bytes 24580
  1207.9 85.7 %copy-start.66 = (f32[256]{0:T(256)S(1)}, f32[256]{0:T(256)}, u32[]{:S(2)}) copy-start(f32[256]{0:T(256)} %copy-done.65) | copy-start | bytes 3076
  1215.2 84.8 %copy-start.68 = (f32[256]{0:T(256)S(1)}, f32[256]{0:T(256)}, u32[]{:S(2)}) copy-start(f32[256]{0:T(256)} %copy-done.67) | copy-start | bytes 3076
  1322.5 30.2 all-to-all-start.7
  1424.2 29.9 all-to-all-start.8
  1454.1 29.7 all-to-all-start.9
  1483.8 28.7 all-to-all-start.10
  1487.3 289.1 %reduce-scatter.15.cloned.1.call-start = ((), (), s32[]{:S(2)}) async-start(), calls=%async_computation.31 | async-start | bytes 1081344
  1563.2 1589.6 %reduce-scatter.13.cloned.1.call-start = ((), (), s32[]{:S(2)}) async-start(), calls=%async_computation.30 | async-start | bytes 69206016
  1674.4 31.4 all-to-all-start.13
  1705.8 57.9 %all-to-all-start.12 = ((bf16[4,64,2048]{2,1,0:T(8,128)(2,1)}), bf16[4,64,2048]{2,1,0:T(8,128)(2,1)}, u32[]{:S(2)}, u32[]{:S(2)}) async-start(bf16[4,64,2048]{2,1,0:T(8,128)(2,1)} %bitcast.463), calls=%async_computation.14 | async-start | bytes 2097152 | tf_op jit(solution)/shard_map/all_to_all | solution.py:275
  1763.7 56.5 %all-to-all-start.11 = ((bf16[4,64,2048]{2,1,0:T(8,128)(2,1)}), bf16[4,64,2048]{2,1,0:T(8,128)(2,1)}, u32[]{:S(2)}, u32[]{:S(2)}) async-start(bf16[4,64,2048]{2,1,0:T(8,128)(2,1)} %bitcast.460), calls=%async_computation.13 | async-start | bytes 2097152 | tf_op jit(solution)/shard_map/all_to_all | solution.py:268
  (76 other events, 1019.0 us)
Sparse Core Ops, SparseCore 0:
  11.0 91.6 all-gather.15
  105.6 86.7 all-gather.13
  195.3 76.0 all-gather.11
  274.3 89.3 all-gather.17
  365.4 52.4 all-gather.21
  485.8 118.1 all-gather.19
  605.8 52.5 all-gather.23
  660.3 54.3 all-gather.25
  728.8 286.7 all-gather.29
  1017.0 78.9 all-gather.27
  1150.6 142.9 reduce-scatter.8
  1297.1 157.6 reduce-scatter.10
  1563.3 138.2 reduce-scatter.14
  1703.9 1448.8 reduce-scatter.12
